TPU v7x, 32 devices: a whole 2x2x4 slice. The times are simulated.
32 devices in a mesh: group: 4 (over x, core), shard: 8 (over z, y).
Axes of the slice: x: 2, y: 2, z: 4, core: 2. Of those that a mesh axis runs over, the one named last changes fastest.
Arguments:
- hidden: bfloat16 [8192, 768], P(('group', 'shard')), may hold values from -40 to 40
- out_grads: bfloat16 [5, 8192, 768], P(None, ('group', 'shard')), may hold values from -40 to 40
- global_inputs: bfloat16 [1024, 768], P(('group', 'shard')), may hold values from -40 to 40
- query_grads: bfloat16 [1024, 768], P(('group', 'shard')), may hold values from -40 to 40
- weight_grads: bfloat16 [6, 768, 768], P(None, 'shard'), may hold values from -48 to 48
- momentum: float32 [6, 768, 768], P(None, 'shard', 'group'), may hold values from -6 to 6
Outputs:
- new_momentum: float32 [6, 768, 768], P(None, 'shard', 'group')
All inputs are finite; a program needn't handle non-finite values. Where the computation divides by a largest or mean magnitude, that divisor is 1e-20 or more.
Results may differ from a plain program's by a relative error of at most 0.0018.
Values may be sent and summed in bfloat16 or wider, within the bound.
A program may use at most 128 MiB of HBM per device.

v0:
```python
import jax
import jax.numpy as jnp
from jax import lax
from jax.sharding import PartitionSpec as P

ITERS = 3
PRECISE = lax.Precision.HIGHEST
DAMPING = 0.1
MOMENTUM = 0.9


def broadcast(array, axis, root):
    mine = lax.axis_index(axis) == root
    return lax.psum(jnp.where(mine, array, jnp.zeros_like(array)), axis)


def outer_sum(matrix_rows):
    return lax.dot_general(
        matrix_rows, matrix_rows, (((0,), (0,)), ((), ())), preferred_element_type=jnp.float32
    )


def on_device(hidden, out_grads, global_inputs, query_grads, weight_grads, momentum):
    model_width = hidden.shape[1]
    group_size = lax.axis_size("group")
    shard_size = lax.axis_size("shard")
    per_group = 8 // group_size
    row_block = model_width // shard_size
    col_block = momentum.shape[2]
    shard_pos = lax.axis_index("shard")
    group_pos = lax.axis_index("group")
    devices = group_size * shard_size
    partials = [outer_sum(hidden), outer_sum(global_inputs)]
    partials = partials + [outer_sum(out_grads[member]) for member in range(5)]
    partials = partials + [outer_sum(query_grads)]
    stacked = jnp.stack([single.astype(jnp.bfloat16) for single in partials])
    summed = lax.psum_scatter(stacked, "group", scatter_dimension=0, tiled=True).astype(jnp.float32)
    factor_ids = group_pos * per_group + jnp.arange(per_group)
    is_global = (factor_ids == 1) | (factor_ids == 7)
    samp_total = float(hidden.shape[0] * devices)
    glob_total = float(global_inputs.shape[0] * devices)
    counted = jnp.where(is_global, glob_total, samp_total).astype(jnp.float32)
    factor_full = lax.psum(summed, "shard")
    covariance = factor_full / counted[:, None, None]
    mean_diag = jnp.trace(covariance, axis1=1, axis2=2) / model_width
    eye_full = jnp.eye(model_width, dtype=jnp.float32)
    matrix = covariance / mean_diag[:, None, None] + DAMPING * eye_full
    row_limit = jnp.max(jnp.sum(jnp.abs(matrix), axis=2), axis=1)
    approx = jnp.broadcast_to(eye_full, matrix.shape) / row_limit[:, None, None]
    for iteration in range(ITERS):
        product = jnp.einsum("kij,kjl->kil", matrix, approx, precision=PRECISE)
        approx = 2.0 * approx - jnp.einsum("kij,kjl->kil", approx, product, precision=PRECISE)
    own_rows = lax.dynamic_slice_in_dim(approx, shard_pos * row_block, row_block, 1)
    all_rows = lax.all_gather(own_rows, "group", axis=0, tiled=True)
    input_inv = jnp.stack(
        [broadcast(approx[factor % per_group], "group", factor // per_group) for factor in range(2)]
    )
    input_cols = lax.dynamic_slice_in_dim(input_inv, group_pos * col_block, col_block, 2)
    out_inverse = all_rows[2:8]
    initial = jnp.zeros(out_inverse.shape, jnp.float32)
    gathered = lax.all_gather(weight_grads, "shard", axis=1, tiled=True)
    columns = lax.slice_in_dim(out_inverse, 0, gathered.shape[1], axis=2)
    left_side = initial + jnp.einsum(
        "wrn,wnd->wrd", columns, gathered.astype(jnp.float32), precision=PRECISE
    )
    local_part = jnp.einsum("wrd,de->wre", left_side[0:5], input_cols[0], precision=PRECISE)
    global_part = jnp.dot(left_side[5], input_cols[1], precision=PRECISE)[None]
    return MOMENTUM * momentum + jnp.concatenate([local_part, global_part], axis=0)


def solution(mesh):
    placed = (
        P(("group", "shard"), None),
        P(None, ("group", "shard"), None),
        P(("group", "shard"), None),
        P(("group", "shard"), None),
        P(None, "shard", None),
        P(None, "shard", "group"),
    )
    return jax.shard_map(
        on_device, mesh=mesh, in_specs=placed, out_specs=P(None, "shard", "group"), check_vma=False
    )
```

profile of v0, /device:TPU:0, one launch (start us, length us, event | category | flops | bytes accessed | tf_op | source)
XLA Modules:
  0.0 529.7 jit_solution(5312361933273675997)
XLA Ops:
  7.4 0.0 copy-start
  7.4 0.0 copy-start.7
  7.4 0.0 reduce-scatter.2.cloned.1.call-start
  7.4 1.0 copy-done
  8.4 1.5 fusion.14
  9.9 2.4 fusion.10
  12.3 0.0 copy-start.6
  12.3 2.7 fusion.16
  15.0 0.0 copy-done.7
  15.0 1.6 fusion.18
  16.6 1.6 fusion.20
  18.1 1.6 fusion.22
  19.7 1.5 fusion.24
  21.2 0.0 copy-done.6
  21.2 1.6 fusion.12
  22.8 0.0 reduce-scatter.2.cloned.1.call-update
  22.9 0.0 all-reduce.4.cloned.1.call-start
  22.9 0.2 iota_compare_fusion
  23.1 0.2 fusion.25
  23.3 1.5 fusion.26
  24.8 79.3 %reduce-scatter.2.cloned.1.call-done = bf16[2,768,768]{2,1,0:T(8,128)(2,1)} async-done(((bf16[8,768,768]{2,1,0:T(8,128)(2,1)}), bf16[2,768,768]{2,1,0:T(8,128)(2,1)}) %reduce-scatter.2.cloned.1.call-update) | async-done | bytes 2359312 | tf_op jit(solution)/shard_map/reduce_scatter | solution.py:37
  104.1 187.7 %all-reduce.5 = f32[2,768,768]{2,1,0:T(8,128)} all-reduce(bf16[2,768,768]{2,1,0:T(8,128)(2,1)} %reduce-scatter.2.cloned.1.call-done), channel_id=1, replica_groups=mesh['group'=4,'shard'=8] {'shard'}, use_global_device_ids=true, to_apply=%region_1.2 | all-reduce | flops 1179648 | bytes 7077888 | tf_op jit(solution)/shard_map/psum | solution.py:43
  291.9 0.0 copy-start.2
  291.9 3.7 select_reduce_fusion
  295.5 0.1 copy-done.2
  295.6 3.0 abs_reduce_fusion
  298.6 0.1 reduce_max.9
  298.7 0.0 copy-start.4
  298.7 0.0 slice-start
  298.7 15.6 %fusion.2 = f32[2,768,768]{2,1,0:T(8,128)S(1)} fusion(f32[2,768,768]{2,1,0:T(8,128)} %get-tuple-element.8, f32[2]{0:T(128)S(1)} %reduce_max.9, f32[768,768]{1,0:T(8,128)} %fusion.26), kind=kOutput, calls=%fused_computation.10 | convolution fusion | flops 10872815616 | bytes 11796488 | tf_op jit(solution)/shard_map/kij,kjl->kil/dot_general | solution.py:51
  314.3 0.0 copy-done.4
  314.3 0.0 slice-start.1
  314.3 12.8 %multiply_subtract_fusion.2 = f32[2,768,768]{2,1,0:T(8,128)S(1)} fusion(f32[2]{0:T(128)S(1)} %reduce_max.9, f32[768,768]{1,0:T(8,128)S(1)} %copy-done.4, f32[2,768,768]{2,1,0:T(8,128)S(1)} %fusion.2), kind=kOutput, calls=%fused_computation.4 | convolution fusion | flops 10876354560 | bytes 11796488 | tf_op jit(solution)/shard_map/kij,kjl->kil/dot_general | solution.py:52
  327.2 0.0 slice-done
  327.2 0.0 slice-done.1
  327.2 12.1 %fusion.40 = f32[2,768,768]{2,1,0:T(8,128)S(1)} fusion(f32[2,768,768]{2,1,0:T(8,128)S(1)} %bitcast.80, f32[2,768,768]{2,1,0:T(8,128)S(1)} %multiply_subtract_fusion.2), kind=kOutput, calls=%fused_computation.65 | convolution fusion | flops 10871635968 | bytes 14155776 | tf_op jit(solution)/shard_map/kij,kjl->kil/dot_general | solution.py:51
  339.3 12.7 %multiply_subtract_fusion.1 = f32[2,768,768]{2,1,0:T(8,128)S(1)} fusion(f32[2,768,768]{2,1,0:T(8,128)S(1)} %multiply_subtract_fusion.2, f32[2,768,768]{2,1,0:T(8,128)S(1)} %fusion.40), kind=kOutput, calls=%fused_computation.3 | convolution fusion | flops 10873995264 | bytes 14155776 | tf_op jit(solution)/shard_map/kij,kjl->kil/dot_general | solution.py:52
  352.0 12.3 %fusion.41 = f32[2,768,768]{2,1,0:T(8,128)S(1)} fusion(f32[2,768,768]{2,1,0:T(8,128)S(1)} %bitcast.80, f32[2,768,768]{2,1,0:T(8,128)S(1)} %multiply_subtract_fusion.1), kind=kOutput, calls=%fused_computation.66 | convolution fusion | flops 10871635968 | bytes 14155776 | tf_op jit(solution)/shard_map/kij,kjl->kil/dot_general | solution.py:51
  364.3 12.5 %multiply_subtract_fusion = f32[2,768,768]{2,1,0:T(8,128)S(1)} fusion(f32[2,768,768]{2,1,0:T(8,128)S(1)} %multiply_subtract_fusion.1, f32[2,768,768]{2,1,0:T(8,128)S(1)} %fusion.41), kind=kOutput, calls=%fused_computation.2 | convolution fusion | flops 10873995264 | bytes 14155776 | tf_op jit(solution)/shard_map/kij,kjl->kil/dot_general | solution.py:52
  376.8 0.0 copy-start.3
  376.8 2.6 slice_select_fusion
  379.4 1.0 copy-done.3
  380.5 0.0 all-reduce.4.cloned.1.call-update
  380.5 0.0 all-gather.5.cloned.1.call-start
  380.5 0.5 all-gather.5.cloned.1.call-update
  381.1 0.0 all-gather.3.cloned.1.call-start
  381.1 1.9 constant_dynamic-slice_fusion
  383.1 0.0 all-gather.3.cloned.1.call-update
  383.1 89.3 %all-reduce.4.cloned.1.call-done = (f32[1,768,768]{2,1,0:T(8,128)}, f32[1,768,768]{2,1,0:T(8,128)}) async-done(((f32[1,768,768]{2,1,0:T(8,128)}, f32[1,768,768]{2,1,0:T(8,128)}), (f32[1,768,768]{2,1,0:T(8,128)}, f32[1,768,768]{2,1,0:T(8,128)})) %all-reduce.4.cloned.1.call-update) | async-done | bytes 4718608 | tf_op jit(solution)/shard_map/psum | solution.py:14
  472.4 2.1 fusion.8
  474.5 0.0 copy-start.5
  474.5 14.5 %all-gather.5.cloned.1.call-done = bf16[6,768,768]{2,1,0:T(8,128)(2,1)} async-done(((bf16[6,96,768]{2,1,0:T(8,128)(2,1)}), bf16[6,768,768]{2,1,0:T(8,128)(2,1)}) %all-gather.5.cloned.1.call-update) | async-done | bytes 7077904 | tf_op jit(solution)/shard_map/all_gather | solution.py:61
  489.0 23.5 %all-gather.3.cloned.1.call-done = f32[8,96,768]{2,1,0:T(8,128)} async-done(((f32[2,96,768]{2,1,0:T(8,128)}), f32[8,96,768]{2,1,0:T(8,128)}) %all-gather.3.cloned.1.call-update) | async-done | bytes 2359312 | tf_op jit(solution)/shard_map/all_gather | solution.py:54
  512.5 0.0 copy-start.1
  512.5 6.7 %fusion.42 = f32[6,96,768]{2,1,0:T(8,128)S(1)} fusion(f32[8,96,768]{2,1,0:T(8,128)} %all-gather.3.cloned.1.call-done, bf16[6,768,768]{2,1,0:T(8,128)(2,1)} %all-gather.5.cloned.1.call-done), kind=kOutput, calls=%fused_computation.67 | convolution fusion | flops 4076863488 | bytes 11206656 | tf_op jit(solution)/shard_map/wrn,wnd->wrd/dot_general | solution.py:63
  519.3 1.3 fusion.29
  520.6 0.5 convolution_bitcast_fusion
  521.1 0.0 copy-done.5
  521.1 0.9 maximum_add_fusion
  522.0 0.0 copy-done.1
  (3 shorter events, 0.0 us)
Async XLA Ops:
  7.4 1.0 copy-start
  7.4 7.6 %copy-start.7 = (bf16[5,256,768]{2,1,0:T(8,128)(2,1)S(1)}, bf16[5,256,768]{2,1,0:T(8,128)(2,1)}, u32[]{:S(2)}) copy-start(bf16[5,256,768]{2,1,0:T(8,128)(2,1)} %param.7) | copy-start | bytes 5898244
  7.4 96.8 %reduce-scatter.2.cloned.1.call-start = ((), (), s32[]{:S(2)}) async-start(), calls=%async_computation.1 | async-start | bytes 11796480 | tf_op jit(solution)/shard_map/reduce_scatter | solution.py:37
  12.3 8.9 %copy-start.6 = (bf16[32,768]{1,0:T(8,128)(2,1)S(1)}, bf16[32,768]{1,0:T(8,128)(2,1)}, u32[]{:S(2)}) copy-start(bf16[32,768]{1,0:T(8,128)(2,1)} %param.9) | copy-start | bytes 147460
  22.9 449.5 %all-reduce.4.cloned.1.call-start = ((), (), s32[]{:S(2)}) async-start(), calls=%async_computation.4 | async-start | bytes 9437184 | tf_op jit(solution)/shard_map/psum | solution.py:14
  291.9 3.8 copy-start.2
  298.7 15.6 %copy-start.4 = (f32[768,768]{1,0:T(8,128)S(1)}, f32[768,768]{1,0:T(8,128)}, u32[]{:S(2)}) copy-start(f32[768,768]{1,0:T(8,128)} %fusion.26) | copy-start | bytes 7077892
  298.7 28.4 %slice-start = ((s8[4718592]{0:T(1024)(128)(4,1)}), s8[4194304]{0:T(1024)(128)(4,1)S(1)}, s32[]{:S(2)}) async-start(s8[4718592]{0:T(1024)(128)(4,1)} %bitcast.79), calls=%async_computation.5 | async-start | bytes 8388608
  314.3 12.9 %slice-start.1 = ((s8[4718592]{0:T(1024)(128)(4,1)}), s8[524288]{0:T(1024)(128)(4,1)S(1)}, s32[]{:S(2)}) async-start(s8[4718592]{0:T(1024)(128)(4,1)} %bitcast.79), calls=%async_computation.6 | async-start | bytes 1048576
  376.8 3.6 copy-start.3
  380.5 108.5 %all-gather.5.cloned.1.call-start = ((), (), s32[]{:S(2)}) async-start(), calls=%async_computation.3 | async-start | bytes 7962624 | tf_op jit(solution)/shard_map/all_gather | solution.py:61
  381.1 131.4 %all-gather.3.cloned.1.call-start = ((), (), s32[]{:S(2)}) async-start(), calls=%async_computation.2 | async-start | bytes 2949120 | tf_op jit(solution)/shard_map/all_gather | solution.py:54
  474.5 46.7 %copy-start.5 = (f32[6,96,192]{2,1,0:T(8,128)S(1)}, f32[6,96,192]{2,1,0:T(8,128)}, u32[]{:S(2)}) copy-start(f32[6,96,192]{2,1,0:T(8,128)} %param.11) | copy-start | bytes 1327108
  512.5 9.5 %copy-start.1 = (bf16[256,768]{1,0:T(8,128)(2,1)S(1)}, bf16[256,768]{1,0:T(8,128)(2,1)}, u32[]{:S(2)}) copy-start(bf16[256,768]{1,0:T(8,128)(2,1)} %param.6) | copy-start | bytes 1179652
Sparse Core Ops, SparseCore 0:
  23.0 81.1 reduce-scatter.1
  380.6 91.7 all-reduce.3
Sparse Core Ops, SparseCore 1:
  383.2 105.8 all-gather.4
  490.4 22.1 all-gather.2
where the time goes:
time: 534 us; the launch traced here: 530 us
  waiting for transfers between devices  207 us (39%)
  blocking collectives  188 us (35%)
  matrix products  101 us (19%)
  between operations  15.3 us (3%)
  other arithmetic  14.3 us (3%)
    psum x1, blocking collectives, on_device(): factor_full = lax.psum(summed, 'shard')  188 us
    psum x1, waiting for transfers between devices, broadcast(): return lax.psum(jnp.where(mine, array, jnp.zeros_like(array)), axis)  89.3 us
    reduce_scatter x1, waiting for transfers between devices, on_device(): lax.psum_scatter(stacked, 'group', scatter_dimension=0, tiled=True)  79.3 us
    dot_general x3, matrix products, on_device(): product = jnp.einsum('kij,kjl->kil', matrix, approx, precision=PRECISE)  39.9 us
    dot_general x3, matrix products, on_device(): jnp.einsum('kij,kjl->kil', approx, product, precision=PRECISE)  38.1 us
    all_gather x1, waiting for transfers between devices, on_device(): all_rows = lax.all_gather(own_rows, 'group', axis=0, tiled=True)  23.5 us
    all_gather x1, waiting for transfers between devices, on_device(): gathered = lax.all_gather(weight_grads, 'shard', axis=1, tiled=True)  14.5 us
    dot_general x8, matrix products, outer_sum(): lax.dot_general(matrix_rows, matrix_rows, (((0,), (0,)), ((), ())), prefe...  14.5 us
  transfers between devices with their start and end apart: 4, of which 4 were waited for; matrix products, arithmetic and copies ran while one was open for 1% of the time, Pallas kernels for 0%

commit v1 on v0

--- a/solution.py
+++ b/solution.py
@@ -40,7 +40,11 @@
     samp_total = float(hidden.shape[0] * devices)
     glob_total = float(global_inputs.shape[0] * devices)
     counted = jnp.where(is_global, glob_total, samp_total).astype(jnp.float32)
-    factor_full = lax.psum(summed, "shard")
+    factor_full = summed
+    for hop in (1, 2, 4):
+        factor_full = factor_full + lax.ppermute(
+            factor_full, "shard", [(dev, dev ^ hop) for dev in range(8)]
+        )
     covariance = factor_full / counted[:, None, None]
     mean_diag = jnp.trace(covariance, axis1=1, axis2=2) / model_width
     eye_full = jnp.eye(model_width, dtype=jnp.float32)

time: 534 us -> 764 us (1.43)
  waiting for transfers between devices: 207 us -> 616 us
  blocking collectives: 188 us -> 0 us
    ppermute x0 -> x3, waiting for transfers between devices: none -> 404 us  [on_device(): lax.ppermute(factor_full, 'shard', [(dev, dev ^ hop) for dev in range(8)])]
    psum x1 -> x0, blocking collectives: 188 us -> none  [on_device(): factor_full = lax.psum(summed, 'shard')]
  transfers between devices with their start and end apart: 4 -> 7, of which waited for: 4 -> 7; matrix products, arithmetic and copies ran while one was open for 1% -> 1% of each run, Pallas kernels for 0% -> 0%
where the time goes in v1:
time: 764 us; the launch traced here: 761 us
  waiting for transfers between devices  616 us (81%)
  matrix products  99.8 us (13%)
  other arithmetic  20 us (3%)
  between operations  15.3 us (2%)
    ppermute x3, waiting for transfers between devices, on_device(): lax.ppermute(factor_full, 'shard', [(dev, dev ^ hop) for dev in range(8)])  404 us
    psum x1, waiting for transfers between devices, broadcast(): return lax.psum(jnp.where(mine, array, jnp.zeros_like(array)), axis)  91.8 us
    reduce_scatter x1, waiting for transfers between devices, on_device(): lax.psum_scatter(stacked, 'group', scatter_dimension=0, tiled=True)  80.8 us
    dot_general x3, matrix products, on_device(): product = jnp.einsum('kij,kjl->kil', matrix, approx, precision=PRECISE)  38.8 us
    dot_general x3, matrix products, on_device(): jnp.einsum('kij,kjl->kil', approx, product, precision=PRECISE)  38 us
    all_gather x1, waiting for transfers between devices, on_device(): all_rows = lax.all_gather(own_rows, 'group', axis=0, tiled=True)  23.5 us
  transfers between devices with their start and end apart: 7, of which 7 were waited for; matrix products, arithmetic and copies ran while one was open for 1% of the time, Pallas kernels for 0%

profile of v1, /device:TPU:0, one launch (start us, length us, event | category | flops | bytes accessed | tf_op | source)
XLA Modules:
  0.0 760.7 jit_solution(5567444273819618124)
XLA Ops:
  7.4 0.0 copy-start
  7.4 0.0 copy-start.6
  7.4 0.0 reduce-scatter.2.cloned.1.call-start
  7.4 1.0 copy-done
  8.4 1.5 fusion.14
  9.9 2.4 fusion.10
  12.3 0.0 copy-start.5
  12.3 2.7 fusion.16
  15.0 0.0 copy-done.6
  15.0 1.5 fusion.18
  16.5 1.5 fusion.20
  18.1 1.6 fusion.22
  19.6 1.6 fusion.24
  21.2 0.0 copy-done.5
  21.2 1.6 fusion.12
  22.8 0.0 reduce-scatter.2.cloned.1.call-update
  22.8 0.5 all-reduce.3.cloned.1.call-start
  23.3 80.8 %reduce-scatter.2.cloned.1.call-done = bf16[2,768,768]{2,1,0:T(8,128)(2,1)} async-done(((bf16[8,768,768]{2,1,0:T(8,128)(2,1)}), bf16[2,768,768]{2,1,0:T(8,128)(2,1)}) %reduce-scatter.2.cloned.1.call-update) | async-done | bytes 2359312 | tf_op jit(solution)/shard_map/reduce_scatter | solution.py:37
  104.1 0.0 copy-start.3
  104.1 2.2 convert_element_type.40
  106.3 1.5 collective-permute-start
  107.8 102.1 %collective-permute-done = f32[2,768,768]{2,1,0:T(8,128)S(1)} collective-permute-done((f32[2,768,768]{2,1,0:T(8,128)S(1)}, f32[2,768,768]{2,1,0:T(8,128)S(1)}, u32[]{:S(2)}, u32[]{:S(2)}) %collective-permute-start) | collective-permute-done | bytes 4718624 | tf_op jit(solution)/shard_map/ppermute | solution.py:45
  209.9 0.0 copy-done.3
  209.9 0.6 convert_add_fusion
  210.5 1.5 collective-permute-start.1
  212.0 101.2 %collective-permute-done.1 = f32[2,768,768]{2,1,0:T(8,128)S(1)} collective-permute-done((f32[2,768,768]{2,1,0:T(8,128)S(1)}, f32[2,768,768]{2,1,0:T(8,128)S(1)}, u32[]{:S(2)}, u32[]{:S(2)}) %collective-permute-start.1) | collective-permute-done | bytes 4718624 | tf_op jit(solution)/shard_map/ppermute | solution.py:45
  313.2 2.7 add.43
  315.9 2.4 collective-permute-start.2
  318.3 0.2 iota_compare_fusion
  318.5 0.2 fusion.25
  318.7 0.2 fusion.26
  318.8 201.2 %collective-permute-done.2 = f32[2,768,768]{2,1,0:T(8,128)} collective-permute-done((f32[2,768,768]{2,1,0:T(8,128)}, f32[2,768,768]{2,1,0:T(8,128)}, u32[]{:S(2)}, u32[]{:S(2)}) %collective-permute-start.2) | collective-permute-done | bytes 4718624 | tf_op jit(solution)/shard_map/ppermute | solution.py:45
  520.0 5.4 select_reduce_fusion
  525.5 2.9 abs_reduce_fusion
  528.3 0.1 reduce_max.9
  528.4 14.5 %fusion.2 = f32[2,768,768]{2,1,0:T(8,128)S(1)} fusion(f32[2,768,768]{2,1,0:T(8,128)} %get-tuple-element.8, f32[2]{0:T(128)S(1)} %reduce_max.9, f32[768,768]{1,0:T(8,128)S(1)} %fusion.26), kind=kOutput, calls=%fused_computation.10 | convolution fusion | flops 10872815616 | bytes 11796488 | tf_op jit(solution)/shard_map/kij,kjl->kil/dot_general | solution.py:55
  543.0 0.0 slice-start.1
  543.0 12.7 %multiply_subtract_fusion.2 = f32[2,768,768]{2,1,0:T(8,128)S(1)} fusion(f32[2]{0:T(128)S(1)} %reduce_max.9, f32[768,768]{1,0:T(8,128)S(1)} %fusion.26, f32[2,768,768]{2,1,0:T(8,128)S(1)} %fusion.2), kind=kOutput, calls=%fused_computation.4 | convolution fusion | flops 10876354560 | bytes 11796488 | tf_op jit(solution)/shard_map/kij,kjl->kil/dot_general | solution.py:56
  555.7 0.0 slice-done
  555.7 0.0 slice-done.1
  555.7 12.1 %fusion.40 = f32[2,768,768]{2,1,0:T(8,128)S(1)} fusion(f32[2,768,768]{2,1,0:T(8,128)S(1)} %bitcast.80, f32[2,768,768]{2,1,0:T(8,128)S(1)} %multiply_subtract_fusion.2), kind=kOutput, calls=%fused_computation.66 | convolution fusion | flops 10871635968 | bytes 14155776 | tf_op jit(solution)/shard_map/kij,kjl->kil/dot_general | solution.py:55
  567.8 12.7 %multiply_subtract_fusion.1 = f32[2,768,768]{2,1,0:T(8,128)S(1)} fusion(f32[2,768,768]{2,1,0:T(8,128)S(1)} %multiply_subtract_fusion.2, f32[2,768,768]{2,1,0:T(8,128)S(1)} %fusion.40), kind=kOutput, calls=%fused_computation.3 | convolution fusion | flops 10873995264 | bytes 14155776 | tf_op jit(solution)/shard_map/kij,kjl->kil/dot_general | solution.py:56
  580.5 12.3 %fusion.41 = f32[2,768,768]{2,1,0:T(8,128)S(1)} fusion(f32[2,768,768]{2,1,0:T(8,128)S(1)} %bitcast.80, f32[2,768,768]{2,1,0:T(8,128)S(1)} %multiply_subtract_fusion.1), kind=kOutput, calls=%fused_computation.67 | convolution fusion | flops 10871635968 | bytes 14155776 | tf_op jit(solution)/shard_map/kij,kjl->kil/dot_general | solution.py:55
  592.8 12.5 %multiply_subtract_fusion = f32[2,768,768]{2,1,0:T(8,128)S(1)} fusion(f32[2,768,768]{2,1,0:T(8,128)S(1)} %multiply_subtract_fusion.1, f32[2,768,768]{2,1,0:T(8,128)S(1)} %fusion.41), kind=kOutput, calls=%fused_computation.2 | convolution fusion | flops 10873995264 | bytes 14155776 | tf_op jit(solution)/shard_map/kij,kjl->kil/dot_general | solution.py:56
  605.4 0.0 copy-start.2
  605.4 2.6 slice_select_fusion
  608.0 1.0 copy-done.2
  609.0 0.0 all-reduce.3.cloned.1.call-update
  609.0 0.0 all-gather.5.cloned.1.call-start
  609.1 0.5 all-gather.5.cloned.1.call-update
  609.6 0.0 all-gather.3.cloned.1.call-start
  609.7 1.9 constant_dynamic-slice_fusion
  611.6 0.0 all-gather.3.cloned.1.call-update
  611.6 91.8 %all-reduce.3.cloned.1.call-done = (f32[1,768,768]{2,1,0:T(8,128)}, f32[1,768,768]{2,1,0:T(8,128)}) async-done(((f32[1,768,768]{2,1,0:T(8,128)}, f32[1,768,768]{2,1,0:T(8,128)}), (f32[1,768,768]{2,1,0:T(8,128)}, f32[1,768,768]{2,1,0:T(8,128)})) %all-reduce.3.cloned.1.call-update) | async-done | bytes 4718608 | tf_op jit(solution)/shard_map/psum | solution.py:14
  703.4 2.1 fusion.8
  705.5 0.0 copy-start.4
  705.5 14.5 %all-gather.5.cloned.1.call-done = bf16[6,768,768]{2,1,0:T(8,128)(2,1)} async-done(((bf16[6,96,768]{2,1,0:T(8,128)(2,1)}), bf16[6,768,768]{2,1,0:T(8,128)(2,1)}) %all-gather.5.cloned.1.call-update) | async-done | bytes 7077904 | tf_op jit(solution)/shard_map/all_gather | solution.py:65
  720.0 23.5 %all-gather.3.cloned.1.call-done = f32[8,96,768]{2,1,0:T(8,128)} async-done(((f32[2,96,768]{2,1,0:T(8,128)}), f32[8,96,768]{2,1,0:T(8,128)}) %all-gather.3.cloned.1.call-update) | async-done | bytes 2359312 | tf_op jit(solution)/shard_map/all_gather | solution.py:58
  743.6 6.7 fusion.42
  750.3 1.3 fusion.29
  751.7 0.5 convolution_bitcast_fusion
  752.2 0.0 copy-done.4
  752.2 0.9 maximum_add_fusion
  753.1 0.0 copy-done.1
  (5 shorter events, 0.0 us)
Async XLA Ops:
  7.4 1.0 copy-start
  7.4 7.6 %copy-start.6 = (bf16[5,256,768]{2,1,0:T(8,128)(2,1)S(1)}, bf16[5,256,768]{2,1,0:T(8,128)(2,1)}, u32[]{:S(2)}) copy-start(bf16[5,256,768]{2,1,0:T(8,128)(2,1)} %param.7) | copy-start | bytes 5898244
  7.4 96.7 %reduce-scatter.2.cloned.1.call-start = ((), (), s32[]{:S(2)}) async-start(), calls=%async_computation.1 | async-start | bytes 11796480 | tf_op jit(solution)/shard_map/reduce_scatter | solution.py:37
  12.3 8.9 %copy-start.5 = (bf16[32,768]{1,0:T(8,128)(2,1)S(1)}, bf16[32,768]{1,0:T(8,128)(2,1)}, u32[]{:S(2)}) copy-start(bf16[32,768]{1,0:T(8,128)(2,1)} %param.9) | copy-start | bytes 147460
  22.8 680.6 %all-reduce.3.cloned.1.call-start = ((), (), s32[]{:S(2)}) async-start(), calls=%async_computation.4 | async-start | bytes 9437184 | tf_op jit(solution)/shard_map/psum | solution.py:14
  104.1 105.8 %copy-start.3 = (bf16[2,768,768]{2,1,0:T(8,128)(2,1)S(1)}, bf16[2,768,768]{2,1,0:T(8,128)(2,1)}, u32[]{:S(2)}) copy-start(bf16[2,768,768]{2,1,0:T(8,128)(2,1)} %reduce-scatter.2.cloned.1.call-done) | copy-start | bytes 7077892
  106.3 103.6 %collective-permute-start = (f32[2,768,768]{2,1,0:T(8,128)S(1)}, f32[2,768,768]{2,1,0:T(8,128)S(1)}, u32[]{:S(2)}, u32[]{:S(2)}) collective-permute-start(f32[2,768,768]{2,1,0:T(8,128)S(1)} %convert_element_type.40), channel_id=1, source_target_pairs={{0,1},{1,0},{2,3},{3,2},{4,5},{5,4},{6,7},{7,6},{8,9},{9,8},{10,11... | collective-permute-start | bytes 14155784 | tf_op jit(solution)/shard_map/ppermute | solution.py:45
  210.5 102.7 %collective-permute-start.1 = (f32[2,768,768]{2,1,0:T(8,128)S(1)}, f32[2,768,768]{2,1,0:T(8,128)S(1)}, u32[]{:S(2)}, u32[]{:S(2)}) collective-permute-start(f32[2,768,768]{2,1,0:T(8,128)S(1)} %convert_add_fusion), channel_id=1, source_target_pairs={{0,2},{1,3},{2,0},{3,1},{4,6},{5,7},{6,4},{7,5},{8,10},{9,11},{10,... | collective-permute-start | bytes 14155784 | tf_op jit(solution)/shard_map/ppermute | solution.py:45
  315.9 204.1 %collective-permute-start.2 = (f32[2,768,768]{2,1,0:T(8,128)}, f32[2,768,768]{2,1,0:T(8,128)}, u32[]{:S(2)}, u32[]{:S(2)}) collective-permute-start(f32[2,768,768]{2,1,0:T(8,128)} %add.43), channel_id=1, source_target_pairs={{0,4},{1,5},{2,6},{3,7},{4,0},{5,1},{6,2},{7,3},{8,12},{9,13},{10,... | collective-permute-start | bytes 14155784 | tf_op jit(solution)/shard_map/ppermute | solution.py:45
  528.4 27.3 %slice-start = ((s8[4718592]{0:T(1024)(128)(4,1)}), s8[4194304]{0:T(1024)(128)(4,1)S(1)}, s32[]{:S(2)}) async-start(s8[4718592]{0:T(1024)(128)(4,1)} %bitcast.79), calls=%async_computation.5 | async-start | bytes 8388608
  543.0 12.8 %slice-start.1 = ((s8[4718592]{0:T(1024)(128)(4,1)}), s8[524288]{0:T(1024)(128)(4,1)S(1)}, s32[]{:S(2)}) async-start(s8[4718592]{0:T(1024)(128)(4,1)} %bitcast.79), calls=%async_computation.6 | async-start | bytes 1048576
  605.4 3.7 copy-start.2
  609.0 111.0 %all-gather.5.cloned.1.call-start = ((), (), s32[]{:S(2)}) async-start(), calls=%async_computation.3 | async-start | bytes 7962624 | tf_op jit(solution)/shard_map/all_gather | solution.py:65
  609.6 134.0 %all-gather.3.cloned.1.call-start = ((), (), s32[]{:S(2)}) async-start(), calls=%async_computation.2 | async-start | bytes 2949120 | tf_op jit(solution)/shard_map/all_gather | solution.py:58
  705.5 46.7 %copy-start.4 = (f32[6,96,192]{2,1,0:T(8,128)S(1)}, f32[6,96,192]{2,1,0:T(8,128)}, u32[]{:S(2)}) copy-start(f32[6,96,192]{2,1,0:T(8,128)} %param.11) | copy-start | bytes 1327108
  743.6 9.5 %copy-start.1 = (bf16[256,768]{1,0:T(8,128)(2,1)S(1)}, bf16[256,768]{1,0:T(8,128)(2,1)}, u32[]{:S(2)}) copy-start(bf16[256,768]{1,0:T(8,128)(2,1)} %param.6) | copy-start | bytes 1179652
Sparse Core Ops, SparseCore 0:
  22.9 81.1 reduce-scatter.1
  609.2 94.2 all-reduce.2
Sparse Core Ops, SparseCore 1:
  611.7 108.3 all-gather.4
  721.5 22.1 all-gather.2
